TPU v7x, 256 devices: a whole 4x4x8 slice. The times are simulated.
256 devices in a mesh: dp: 2 (over core), seq: 8 (over z), expert: 16 (over y, x).
Axes of the slice: x: 4, y: 4, z: 8, core: 2. Of those that a mesh axis runs over, the one named last changes fastest.
Arguments:
- tokens: bfloat16 [16384, 2048], P(('dp', 'seq')), may hold values from -6 to 6
- phi: bfloat16 [2048, 32], P(None, 'expert'), may hold values from -40 to 40
- w_in: bfloat16 [32, 2048, 8192], P('expert', None, ('dp', 'seq')), may hold values from -1 to 1
- w_out: bfloat16 [32, 8192, 2048], P('expert', ('dp', 'seq')), may hold values from -0.25 to 0.25
Outputs:
- mixed: bfloat16 [16384, 2048], P(('dp', 'seq', 'expert'))
All inputs are finite; a program needn't handle non-finite values.
Results may differ from a plain program's by a relative error of at most 0.0068.
Values may be sent and summed in bfloat16 or wider, within the bound.
A program may use at most 64 MiB of HBM per device.

v0:
```python
import jax
import jax.numpy as jnp
from jax import lax
from jax.sharding import PartitionSpec as P


def on_device(tokens, phi, w_in, w_out):
    logits = lax.dot_general(
        phi, tokens, (((0,), (1,)), ((), ())), preferred_element_type=jnp.float32
    )
    slot_max = lax.pmax(jnp.max(logits, axis=1), "seq")
    spread = jnp.exp(logits - slot_max[:, None])
    numerator = jnp.dot(spread.astype(jnp.bfloat16), tokens, preferred_element_type=jnp.float32)
    denominator = jnp.sum(spread, axis=1)
    numer_seq, denom_seq = lax.psum((numerator, denominator), "seq")
    own_slots = (numer_seq / denom_seq[:, None]).astype(jnp.bfloat16)
    slot_in = lax.all_gather(own_slots[None], "dp", axis=0, tiled=True)
    hidden = jax.nn.gelu(
        jnp.einsum("ced,edf->cef", slot_in, w_in, preferred_element_type=jnp.float32),
        approximate=True,
    ).astype(jnp.bfloat16)
    partial_value = jnp.einsum("cef,efd->ced", hidden, w_out, preferred_element_type=jnp.float32)
    totals = lax.psum(partial_value, ("dp", "seq"))
    summed = lax.dynamic_index_in_dim(totals, lax.axis_index("dp"), 0, keepdims=False)
    slot_out = summed.astype(jnp.bfloat16)
    row_max = lax.pmax(jnp.max(logits, axis=0), "expert")
    combine_weights = jnp.exp(logits - row_max[None, :])
    local_numer = lax.dot_general(
        combine_weights.astype(jnp.bfloat16),
        slot_out,
        (((0,), (0,)), ((), ())),
        preferred_element_type=jnp.float32,
    )
    mixed_numer, mixed_denom = (
        lax.psum_scatter(local_numer, "expert", scatter_dimension=0, tiled=True),
        lax.psum_scatter(
            jnp.sum(combine_weights, axis=0), "expert", scatter_dimension=0, tiled=True
        ),
    )
    return (mixed_numer / mixed_denom[:, None]).astype(jnp.bfloat16)


def solution(mesh):
    placed = (
        P(("dp", "seq"), None),
        P(None, "expert"),
        P("expert", None, ("dp", "seq")),
        P("expert", ("dp", "seq"), None),
    )
    return jax.shard_map(
        on_device,
        mesh=mesh,
        in_specs=placed,
        out_specs=P(("dp", "seq", "expert"), None),
        check_vma=False,
    )
```

profile of v0, /device:TPU:2, one launch (start us, length us, event | category | flops | bytes accessed | tf_op | source)
XLA Modules:
  0.0 258.3 jit_solution(14364468299653725748)
XLA Ops:
  6.5 0.0 copy-start
  6.5 0.0 reduce-scatter.2.cloned.1.call-start
  6.5 0.7 copy-done
  7.2 3.5 %fusion.35 = (f32[1024]{0:T(1024)S(1)}, f32[2]{0:T(128)S(1)}, f32[2,1024]{1,0:T(2,128)S(1)}) fusion(bf16[2048,2]{0,1:T(2,128)(2,1)S(1)} %copy-done, bf16[1024,2048]{1,0:T(8,128)(2,1)} %param.4), kind=kOutput, calls=%fused_computation.35 | convolution fusion | flops 8391678 | bytes 4214792 | tf_op jit(solution)/shard_map/dot_general | solution.py:8
  10.7 37.7 %pmax.14 = f32[1024]{0:T(1024)S(1)} all-reduce(f32[1024]{0:T(1024)S(1)} %get-tuple-element.7), channel_id=1, replica_groups=mesh['dp'=2,'seq'=8,'expert'=16] {'expert'}, use_global_device_ids=true, to_apply=%region_1.0 | all-reduce | flops 1024 | bytes 8192 | tf_op jit(solution)/shard_map/pmax | solution.py:26
  48.4 19.0 %pmax.15 = f32[2]{0:T(128)S(1)} all-reduce(f32[2]{0:T(128)S(1)} %get-tuple-element.8), channel_id=1, replica_groups=mesh['dp'=2,'seq'=8,'expert'=16] {'seq'}, use_global_device_ids=true, to_apply=%region_3.0 | all-reduce | flops 2 | bytes 16 | tf_op jit(solution)/shard_map/pmax | solution.py:11
  67.4 2.9 %fusion.23 = f32[2,2048]{1,0:T(2,128)S(1)} fusion(bf16[1024,2048]{1,0:T(8,128)(2,1)} %param.4, f32[2,1024]{1,0:T(2,128)S(1)} %get-tuple-element.11, f32[2]{0:T(128)S(1)} %pmax.15), kind=kOutput, calls=%fused_computation.25 | convolution fusion | flops 8392704 | bytes 4218888 | tf_op jit(solution)/shard_map/dot_general | solution.py:13
  70.3 0.2 fusion.19
  70.5 27.1 %all-reduce.1 = (f32[2,2048]{1,0:T(2,128)S(1)}, f32[2]{0:T(128)S(1)}) all-reduce(f32[2,2048]{1,0:T(2,128)S(1)} %fusion.23, f32[2]{0:T(128)S(1)} %get-tuple-element.6), channel_id=1, replica_groups=mesh['dp'=2,'seq'=8,'expert'=16] {'seq'}, use_global_device_ids=true, to_apply=%region_4.0 | all-reduce | flops 4098 | bytes 32784 | tf_op jit(solution)/shard_map/psum | solution.py:15
  97.6 0.1 fusion.18
  97.6 1.8 all-gather.1
  99.4 4.7 %convolution_bitcast_fusion = f32[2,2,2048]{2,0,1:T(2,128)S(1)} fusion(bf16[2,512,2048]{2,1,0:T(8,128)(2,1)} %param.7, bf16[2,2048,512]{2,1,0:T(8,128)(2,1)} %param.6, bf16[2,2,2048]{2,1,0:T(2,128)(2,1)S(1)} %all-gather.1), kind=kOutput, calls=%fused_computation | convolution fusion | flops 16795648 | bytes 8437760 | tf_op jit(solution)/shard_map/cef,efd->ced/dot_general | solution.py:22
  104.1 50.2 %psum.23 = bf16[2,2,2048]{2,0,1:T(2,128)(2,1)S(1)} all-reduce(f32[2,2,2048]{2,0,1:T(2,128)S(1)} %convolution_bitcast_fusion), channel_id=1, replica_groups=mesh['dp'=2,'seq'=8,'expert'=16] {'dp','seq'}, use_global_device_ids=true, to_apply=%region_7.8 | all-reduce | flops 8192 | bytes 49152 | tf_op jit(solution)/shard_map/psum | solution.py:23
  154.3 4.5 %fusion.15 = f32[1024,2048]{1,0:T(8,128)} fusion(bf16[1,2,2048]{2,0,1:T(2,128)(2,1)S(1)} %dynamic-slice_convert_fusion, f32[2,1024]{1,0:T(2,128)S(1)} %get-tuple-element.11, f32[1024]{0:T(1024)S(1)} %pmax.14), kind=kOutput, calls=%fused_computation.15 | convolution fusion | flops 8392704 | bytes 8409088 | tf_op jit(solution)/shard_map/dot_general | solution.py:28
  158.9 0.0 copy-start.1
  158.9 0.0 reduce-scatter.2.cloned.1.call-update
  158.9 0.6 copy-done.1
  159.5 0.6 dynamic-slice
  160.8 40.2 %all-reduce = f32[1024]{0:T(1024)S(1)} all-reduce(f32[1024]{0:T(1024)S(1)} %get-tuple-element.5), channel_id=4, replica_groups=mesh['dp'=2,'seq'=8,'expert'=16] {'expert'}, use_global_device_ids=true, to_apply=%region_10.11.clone | all-reduce | flops 1024 | bytes 8192
  201.0 0.1 dynamic-slice.1
  201.1 48.5 %reduce-scatter.2.cloned.1.call-done = f32[64,2048]{1,0:T(8,128)} async-done(((f32[1024,2048]{1,0:T(8,128)}), f32[64,2048]{1,0:T(8,128)}) %reduce-scatter.2.cloned.1.call-update) | async-done | bytes 524304 | tf_op jit(solution)/shard_map/reduce_scatter | solution.py:35
  249.6 1.8 divide_convert_fusion
  (1 shorter events, 0.0 us)
Async XLA Ops:
  6.5 0.7 copy-start
  6.5 243.0 %reduce-scatter.2.cloned.1.call-start = ((), (), s32[]{:S(2)}) async-start(), calls=%async_computation.1 | async-start | bytes 8912896 | tf_op jit(solution)/shard_map/reduce_scatter | solution.py:35
  158.9 0.7 copy-start.1
Sparse Core Ops, SparseCore 0:
  159.0 90.5 reduce-scatter.1
where the time goes:
time: 259 us; the launch traced here: 258 us
  blocking collectives  176 us (68%)
  waiting for transfers between devices  48.5 us (19%)
  matrix products  15.6 us (6%)
  between operations  14.1 us (5%)
    psum x1, blocking collectives, on_device(): totals = lax.psum(partial_value, ('dp', 'seq'))  50.2 us
    reduce_scatter x1, waiting for transfers between devices, on_device(): lax.psum_scatter(local_numer, 'expert', scatter_dimension=0, tiled=True)  48.5 us
    unnamed x1, blocking collectives  40.2 us
    pmax x1, blocking collectives, on_device(): row_max = lax.pmax(jnp.max(logits, axis=0), 'expert')  37.7 us
    psum x1, blocking collectives, on_device(): numer_seq, denom_seq = lax.psum((numerator, denominator), 'seq')  27.1 us
    pmax x1, blocking collectives, on_device(): slot_max = lax.pmax(jnp.max(logits, axis=1), 'seq')  19 us
  transfers between devices with their start and end apart: 1, of which 1 were waited for; matrix products, arithmetic and copies ran while one was open for 0% of the time, Pallas kernels for 0%

commit v1 on v0

--- a/solution.py
+++ b/solution.py
@@ -20,7 +20,9 @@
         approximate=True,
     ).astype(jnp.bfloat16)
     partial_value = jnp.einsum("cef,efd->ced", hidden, w_out, preferred_element_type=jnp.float32)
-    totals = lax.psum(partial_value, ("dp", "seq"))
+    totals = partial_value
+    for axis in ("seq", "dp"):
+        totals = lax.psum(totals, axis)
     summed = lax.dynamic_index_in_dim(totals, lax.axis_index("dp"), 0, keepdims=False)
     slot_out = summed.astype(jnp.bfloat16)
     row_max = lax.pmax(jnp.max(logits, axis=0), "expert")

time: 259 us -> 236 us (0.911)
  blocking collectives: 176 us -> 157 us
  waiting for transfers between devices: 48.5 us -> 45.5 us
    psum x1 -> x2, blocking collectives: 50.2 us -> 30.9 us  [on_device(): totals = lax.psum(totals, axis)]
    reduce_scatter x1, waiting for transfers between devices: 48.5 us -> 45.5 us  [on_device(): lax.psum_scatter(local_numer, 'expert', scatter_dimension=0, tiled=True)]
where the time goes in v1:
time: 236 us
  blocking collectives  157 us (67%)
  waiting for transfers between devices  45.5 us (19%)
  matrix products  15.6 us (7%)
  between operations  14.1 us (6%)
    reduce_scatter x1, waiting for transfers between devices, on_device(): lax.psum_scatter(local_numer, 'expert', scatter_dimension=0, tiled=True)  45.5 us
    unnamed x1, blocking collectives  40.2 us
    pmax x1, blocking collectives, on_device(): row_max = lax.pmax(jnp.max(logits, axis=0), 'expert')  37.7 us
    psum x2, blocking collectives, on_device(): totals = lax.psum(totals, axis)  30.9 us
    psum x1, blocking collectives, on_device(): numer_seq, denom_seq = lax.psum((numerator, denominator), 'seq')  27.1 us
    pmax x1, blocking collectives, on_device(): slot_max = lax.pmax(jnp.max(logits, axis=1), 'seq')  19 us
  transfers between devices with their start and end apart: 1, of which 1 were waited for; matrix products, arithmetic and copies ran while one was open for 0% of the time, Pallas kernels for 0%

profile of v1, /device:TPU:2, one launch (start us, length us, event | category | flops | bytes accessed | tf_op | source)
XLA Modules:
  0.0 236.0 jit_solution(6344803138465717594)
XLA Ops:
  6.5 0.0 copy-start
  6.5 0.0 reduce-scatter.2.cloned.1.call-start
  6.5 0.7 copy-done
  7.2 3.5 %fusion.35 = (f32[1024]{0:T(1024)S(1)}, f32[2]{0:T(128)S(1)}, f32[2,1024]{1,0:T(2,128)S(1)}) fusion(bf16[2048,2]{0,1:T(2,128)(2,1)S(1)} %copy-done, bf16[1024,2048]{1,0:T(8,128)(2,1)} %param.4), kind=kOutput, calls=%fused_computation.35 | convolution fusion | flops 8391678 | bytes 4214792 | tf_op jit(solution)/shard_map/dot_general | solution.py:8
  10.7 37.7 %pmax.14 = f32[1024]{0:T(1024)S(1)} all-reduce(f32[1024]{0:T(1024)S(1)} %get-tuple-element.7), channel_id=1, replica_groups=mesh['dp'=2,'seq'=8,'expert'=16] {'expert'}, use_global_device_ids=true, to_apply=%region_1.0 | all-reduce | flops 1024 | bytes 8192 | tf_op jit(solution)/shard_map/pmax | solution.py:28
  48.4 19.0 %pmax.15 = f32[2]{0:T(128)S(1)} all-reduce(f32[2]{0:T(128)S(1)} %get-tuple-element.8), channel_id=1, replica_groups=mesh['dp'=2,'seq'=8,'expert'=16] {'seq'}, use_global_device_ids=true, to_apply=%region_3.0 | all-reduce | flops 2 | bytes 16 | tf_op jit(solution)/shard_map/pmax | solution.py:11
  67.4 2.9 %fusion.23 = f32[2,2048]{1,0:T(2,128)S(1)} fusion(bf16[1024,2048]{1,0:T(8,128)(2,1)} %param.4, f32[2,1024]{1,0:T(2,128)S(1)} %get-tuple-element.11, f32[2]{0:T(128)S(1)} %pmax.15), kind=kOutput, calls=%fused_computation.25 | convolution fusion | flops 8392704 | bytes 4218888 | tf_op jit(solution)/shard_map/dot_general | solution.py:13
  70.3 0.2 fusion.19
  70.5 27.1 %all-reduce.1 = (f32[2,2048]{1,0:T(2,128)S(1)}, f32[2]{0:T(128)S(1)}) all-reduce(f32[2,2048]{1,0:T(2,128)S(1)} %fusion.23, f32[2]{0:T(128)S(1)} %get-tuple-element.6), channel_id=1, replica_groups=mesh['dp'=2,'seq'=8,'expert'=16] {'seq'}, use_global_device_ids=true, to_apply=%region_4.0 | all-reduce | flops 4098 | bytes 32784 | tf_op jit(solution)/shard_map/psum | solution.py:15
  97.6 0.1 fusion.18
  97.6 1.8 all-gather.1
  99.4 4.7 %convolution_bitcast_fusion = f32[2,2,2048]{2,0,1:T(2,128)S(1)} fusion(bf16[2,512,2048]{2,1,0:T(8,128)(2,1)} %param.7, bf16[2,2048,512]{2,1,0:T(8,128)(2,1)} %param.6, bf16[2,2,2048]{2,1,0:T(2,128)(2,1)S(1)} %all-gather.1), kind=kOutput, calls=%fused_computation | convolution fusion | flops 16795648 | bytes 8437760 | tf_op jit(solution)/shard_map/cef,efd->ced/dot_general | solution.py:22
  104.1 27.6 %psum.30 = f32[2,2,2048]{2,0,1:T(2,128)S(1)} all-reduce(f32[2,2,2048]{2,0,1:T(2,128)S(1)} %convolution_bitcast_fusion), channel_id=1, replica_groups=mesh['dp'=2,'seq'=8,'expert'=16] {'seq'}, use_global_device_ids=true, to_apply=%region_7.8 | all-reduce | flops 8192 | bytes 65536 | tf_op jit(solution)/shard_map/psum | solution.py:25
  131.6 3.4 %psum.31 = bf16[2,2,2048]{2,0,1:T(2,128)(2,1)S(1)} all-reduce(f32[2,2,2048]{2,0,1:T(2,128)S(1)} %psum.30), channel_id=1, replica_groups=mesh['dp'=2,'seq'=8,'expert'=16] {'dp'}, use_global_device_ids=true, to_apply=%region_8.9 | all-reduce | flops 8192 | bytes 49152 | tf_op jit(solution)/shard_map/psum | solution.py:25
  135.1 4.5 %fusion.15 = f32[1024,2048]{1,0:T(8,128)} fusion(bf16[1,2,2048]{2,0,1:T(2,128)(2,1)S(1)} %dynamic-slice_convert_fusion, f32[2,1024]{1,0:T(2,128)S(1)} %get-tuple-element.11, f32[1024]{0:T(1024)S(1)} %pmax.14), kind=kOutput, calls=%fused_computation.15 | convolution fusion | flops 8392704 | bytes 8409088 | tf_op jit(solution)/shard_map/dot_general | solution.py:30
  139.6 0.0 copy-start.1
  139.6 0.0 reduce-scatter.2.cloned.1.call-update
  139.6 0.6 copy-done.1
  140.3 0.6 dynamic-slice
  141.5 40.2 %all-reduce = f32[1024]{0:T(1024)S(1)} all-reduce(f32[1024]{0:T(1024)S(1)} %get-tuple-element.5), channel_id=4, replica_groups=mesh['dp'=2,'seq'=8,'expert'=16] {'expert'}, use_global_device_ids=true, to_apply=%region_11.12.clone | all-reduce | flops 1024 | bytes 8192
  181.7 0.1 dynamic-slice.1
  181.8 45.5 %reduce-scatter.2.cloned.1.call-done = f32[64,2048]{1,0:T(8,128)} async-done(((f32[1024,2048]{1,0:T(8,128)}), f32[64,2048]{1,0:T(8,128)}) %reduce-scatter.2.cloned.1.call-update) | async-done | bytes 524304 | tf_op jit(solution)/shard_map/reduce_scatter | solution.py:37
  227.3 1.8 divide_convert_fusion
  (1 shorter events, 0.0 us)
Async XLA Ops:
  6.5 0.7 copy-start
  6.5 220.8 %reduce-scatter.2.cloned.1.call-start = ((), (), s32[]{:S(2)}) async-start(), calls=%async_computation.1 | async-start | bytes 8912896 | tf_op jit(solution)/shard_map/reduce_scatter | solution.py:37
  139.6 0.7 copy-start.1
Sparse Core Ops, SparseCore 0:
  139.8 87.5 reduce-scatter.1
